TPU v7x, 128 devices: a whole 4x4x4 slice. The times are simulated.
128 devices in a mesh: pts: 16 (over z, y), freq: 8 (over x, core).
Axes of the slice: x: 4, y: 4, z: 4, core: 2. Of those that a mesh axis runs over, the one named last changes fastest.
Arguments:
- spectra: bfloat16 [128, 5, 4096, 128], P('freq', None, 'pts'), parts along dimension 0, may hold values from -200 to 200, as said below
- weights: float32 [4096], P('pts'), as said below
Outputs:
- mode_shapes: bfloat16 [128, 5, 4096, 128], P('freq', None, 'pts'), parts along dimension 0
There are 8 independent parts, one for each index of `freq`. A program takes and returns all parts, laid end to end along the dimension named above; an argument that names none is the same for every part. Nothing has to cross between parts.
Inputs may be any that keep to these rules, and one draw needn't show every extreme that they name: `spectra`: each row (frequency, variable, point) and each block's column pair has its own scale; the complex columns are independent. `weights`: Positive; their sum is of order one.
All inputs are finite; a program needn't handle non-finite values.
Results may differ from a plain program's by a relative error of at most 0.0054.
Values sent between devices are 32-bit elements; how exact they have to be, the bound alone decides.
No kernel may reach another device: no remote copies, remote signals or barrier semaphores. Data moves between devices by JAX's collectives and lax.ppermute only.
A program may use at most 64 MiB of HBM per device.

v0:
```python
import jax
import jax.numpy as jnp
from jax import lax
from jax.sharding import PartitionSpec as P

NS_STEPS = 10


def split_parts(products):
    half_cols = products.shape[-1] // 2
    top_left = products[:, :half_cols, :half_cols]
    top_right = products[:, :half_cols, half_cols:]
    bottom_left = products[:, half_cols:, :half_cols]
    bottom_right = products[:, half_cols:, half_cols:]
    return (top_left + bottom_right, top_right - bottom_left)


def build_cross(real_part, imag_part):
    upper_row = jnp.concatenate([real_part, imag_part], 2)
    lower_row = jnp.concatenate([-imag_part, real_part], 2)
    return jnp.concatenate([upper_row, lower_row], 1)


def upper_of(cross_gram):
    order = cross_gram.shape[-1]
    places = jnp.arange(order)

    def eliminate(column, carry):
        working, factor = carry
        picker = (places == column).astype(jnp.float32)
        below = (places >= column).astype(jnp.float32)
        current = jnp.sum(working * picker[None, None, :], axis=2) * below[None, :]
        pivot = jnp.sqrt(jnp.sum(current * picker[None, :], axis=1))
        scaled = current / pivot[:, None]
        factor = factor + scaled[:, None, :] * picker[None, :, None]
        working = working - scaled[:, :, None] * scaled[:, None, :]
        return (working, factor)

    start = (cross_gram, jnp.zeros_like(cross_gram))
    working, factor = lax.fori_loop(0, order, eliminate, start)
    return factor


def solve_upper(upper_factor, right_side):
    order = upper_factor.shape[-1]
    places = jnp.arange(order)

    def back_step(count, solved):
        row = order - 1 - count
        picker = (places == row).astype(jnp.float32)
        factor_row = jnp.sum(upper_factor * picker[None, :, None], axis=1)
        side_row = jnp.sum(right_side * picker[None, :, None], axis=1)
        pivot = jnp.sum(factor_row * picker[None, :], axis=1)
        known = jnp.einsum("fj,fjk->fk", factor_row, solved, precision=lax.Precision.HIGHEST)
        value = (side_row - known) / pivot[:, None]
        return solved + picker[None, :, None] * value[:, None, :]

    return lax.fori_loop(0, order, back_step, jnp.zeros_like(right_side))


def gram_of(upper_factor):
    return jnp.einsum("fki,fkj->fij", upper_factor, upper_factor, precision=lax.Precision.HIGHEST)


def local(spectra, weights):
    freq_count, var_count, point_count, col_count = spectra.shape
    root_weights = jnp.sqrt(weights)
    weighted = (root_weights[None, None, :, None] * spectra.astype(jnp.float32)).astype(
        jnp.bfloat16
    )
    flat_rows = weighted.reshape(freq_count, var_count * point_count, col_count)
    products = jnp.einsum("frc,frd->fcd", flat_rows, flat_rows, preferred_element_type=jnp.float32)
    real_part, imag_part = split_parts(products)
    cross_gram = build_cross(real_part, imag_part)
    summed = lax.psum(cross_gram, "pts")
    upper_factor = upper_of(summed)
    frob_norm = jnp.sqrt(jnp.sum(upper_factor * upper_factor, axis=(1, 2)))
    polar = upper_factor / frob_norm[:, None, None]
    for sweep in range(NS_STEPS):
        inner_gram = gram_of(polar)
        polar = 1.5 * polar - 0.5 * jnp.einsum(
            "fij,fjk->fik", polar, inner_gram, precision=lax.Precision.HIGHEST
        )
    mapping = solve_upper(upper_factor, polar).astype(jnp.bfloat16)
    shapes = jnp.einsum("fvpc,fcd->fvpd", spectra, mapping, preferred_element_type=jnp.float32)
    return shapes.astype(jnp.bfloat16)


def solution(mesh):
    in_specs = (P("freq", None, "pts", None), P("pts"))
    out_specs = P("freq", None, "pts", None)
    return jax.shard_map(local, mesh=mesh, in_specs=in_specs, out_specs=out_specs, check_vma=False)
```

profile of v0, /device:TPU:0, one launch (start us, length us, event | category | flops | bytes accessed | tf_op | source)
XLA Modules:
  0.0 935.5 jit_solution(8490604428545319796)
XLA Ops:
  7.2 4.0 multiply_convert_fusion
  14.6 90.1 %all-reduce.2.cloned.1.call-done = f32[16,128,128]{2,1,0:T(8,128)} async-done(((f32[16,128,128]{2,1,0:T(8,128)}), f32[16,128,128]{2,1,0:T(8,128)}) %all-reduce.2.cloned.1.call-update) | async-done | bytes 1048592 | tf_op jit(solution)/shard_map/psum | solution.py:75
  104.7 568.0 %while.32 = (s32[]{:T(128)}, f32[16,128,128]{2,1,0:T(8,128)}, f32[16,128,128]{2,1,0:T(8,128)S(1)}, s32[]{:T(128)}, s32[]{:T(128)}) while((s32[]{:T(128)}, f32[16,128,128]{2,1,0:T(8,128)}, f32[16,128,128]{2,1,0:T(8,128)S(1)}, s32[]{:T(128)}, s32[]{:T(128)}) %tuple.73), condition=%wide.region_4.0_spmd.clone.clone, body=%wide.region_1.0_spmd.clone.clone.sunk | while | flops 1843699 | bytes 5287763 | solution.py:40
  106.5 2.7 select_add_fusion.2
  110.9 2.7 select_add_fusion.2
  115.3 2.7 select_add_fusion.2
  124.2 2.7 select_add_fusion.2
  133.1 2.7 select_add_fusion.2
  137.5 2.7 select_add_fusion.2
  141.9 2.7 select_add_fusion.2
  146.4 2.7 select_add_fusion.2
  150.8 2.7 select_add_fusion.2
  155.2 2.7 select_add_fusion.2
  159.7 2.7 select_add_fusion.2
  164.1 2.7 select_add_fusion.2
  168.5 2.7 select_add_fusion.2
  173.0 2.7 select_add_fusion.2
  177.4 2.7 select_add_fusion.2
  181.8 2.7 select_add_fusion.2
  186.3 2.7 select_add_fusion.2
  190.7 2.7 select_add_fusion.2
  195.1 2.7 select_add_fusion.2
  199.6 2.7 select_add_fusion.2
  208.4 2.7 select_add_fusion.2
  217.3 2.7 select_add_fusion.2
  221.7 2.7 select_add_fusion.2
  226.2 2.7 select_add_fusion.2
  230.6 2.7 select_add_fusion.2
  235.0 2.7 select_add_fusion.2
  705.7 208.5 %while.31 = (s32[]{:T(128)}, f32[16,128,128]{2,1,0:T(8,128)S(1)}, f32[16,128,128]{2,1,0:T(8,128)S(1)}, f32[16,128,128]{2,1,0:T(8,128)S(1)}, s32[]{:T(128)}, /*index=5*/s32[]{:T(128)}, s32[]{:T(128)}) while((s32[]{:T(128)}, f32[16,128,128]{2,1,0:T(8,128)S(1)}, f32[16,128,128]{2,1,0:T(8,128)S(1)}, f32[16,128,128]{2,1,0:T(8,128)S(1)}, ...), condition=%wide.region_10.0_spmd.clone, body=%wide.region_6.0_spmd.clone.sunk | while | flops 5247220 | bytes 5318896 | solution.py:58
  914.2 6.4 convert_bitcast_fusion
  920.6 7.8 copy.8
  (1540 shorter events, 737.8 us)
Async XLA Ops:
  6.5 98.1 %all-reduce.2.cloned.1.call-start = ((), (), s32[]{:S(2)}) async-start(), calls=%async_computation | async-start | bytes 2097152 | tf_op jit(solution)/shard_map/psum | solution.py:75
Sparse Core Ops, SparseCore 0:
  14.7 89.9 all-reduce.1
where the time goes:
time: 950 us; the launch traced here: 936 us
  other arithmetic  655 us (69%)
  matrix products  160 us (17%)
  waiting for transfers between devices  90.1 us (9%)
  between operations  13.8 us (1%)
  local copies, waits for them, and re-layouts  9.6 us (1%)
    add x128, other arithmetic, eliminate(): factor = factor + scaled[:, None, :] * picker[None, :, None]  340 us
    reduce_sum x128, other arithmetic, eliminate(): current = jnp.sum(working * picker[None, None, :], axis=2) * below[None, :]  200 us
    dot_general x128, matrix products, back_step(): jnp.einsum('fj,fjk->fk', factor_row, solved, precision=lax.Precision.HIGH...  120 us
    psum x1, waiting for transfers between devices, local(): summed = lax.psum(cross_gram, 'pts')  90.1 us
    reduce_sum x128, other arithmetic, back_step(): factor_row = jnp.sum(upper_factor * picker[None, :, None], axis=1)  33.5 us
    add x128, other arithmetic, back_step(): return solved + picker[None, :, None] * value[:, None, :]  25.6 us
    dot_general x10, matrix products, gram_of(): jnp.einsum('fki,fkj->fij', upper_factor, upper_factor, precision=lax.Prec...  19.4 us
  transfers between devices with their start and end apart: 1, of which 1 were waited for; matrix products, arithmetic and copies ran while one was open for 0% of the time, Pallas kernels for 0%

commit v1 on v0

v1 whole, which is shorter than its diff:
```python
import jax
import jax.numpy as jnp
from jax import lax
from jax.experimental import pallas as pl
from jax.experimental.pallas import tpu as pltpu
from jax.sharding import PartitionSpec as P

NS_STEPS = 10
HALF = 64
COLS = 2 * HALF


def places():
    rows = lax.broadcasted_iota(jnp.int32, (HALF, HALF), 0)
    cols = lax.broadcasted_iota(jnp.int32, (HALF, HALF), 1)
    return rows, cols


def pack(real_part, imag_part):
    rows, cols = places()
    square = jnp.where(rows >= cols, real_part, imag_part)
    return jnp.concatenate([square[: HALF // 2], square[HALF // 2 :]], 1)


def unpack(packed):
    rows, cols = places()
    square = jnp.concatenate([packed[:, :HALF], packed[:, HALF:]], 0)
    flipped = square.T
    real_part = jnp.where(rows >= cols, square, flipped)
    imag_part = jnp.where(rows < cols, square, jnp.where(rows > cols, -flipped, 0.0))
    return real_part, imag_part


def real_form(real_part, imag_part):
    upper_row = jnp.concatenate([real_part, imag_part], 1)
    lower_row = jnp.concatenate([-imag_part, real_part], 1)
    return jnp.concatenate([upper_row, lower_row], 0)


def gram_kernel(spectra_ref, weights_ref, packed_ref, root_ref):
    @pl.when(pl.program_id(0) == 0)
    def _():
        for part in range(weights_ref.shape[0]):
            row = jnp.sqrt(weights_ref[part : part + 1, :])
            root_ref[part * COLS : (part + 1) * COLS, :] = jnp.broadcast_to(row, (COLS, COLS)).T

    for spot in range(spectra_ref.shape[0]):
        weighted = (root_ref[...][None] * spectra_ref[spot].astype(jnp.float32)).astype(jnp.bfloat16)
        rows = weighted.reshape(-1, COLS)
        products = lax.dot_general(
            rows, rows, (((0,), (0,)), ((), ())), preferred_element_type=jnp.float32
        )
        real_part = products[:HALF, :HALF] + products[HALF:, HALF:]
        imag_part = products[:HALF, HALF:] - products[HALF:, :HALF]
        packed_ref[spot] = pack(real_part, imag_part)


def split(value):
    high = value.astype(jnp.bfloat16)
    low = (value - high.astype(jnp.float32)).astype(jnp.bfloat16)
    return high, low


def left_of(value):
    return jnp.concatenate(split(value), 1)


def right_of(value):
    row = jnp.concatenate(split(value), 1)
    return jnp.concatenate([row, row], 0)


def product(left, right):
    both = jnp.dot(left, right, preferred_element_type=jnp.float32)
    return both[:, :COLS] + both[:, COLS:]


def polar_kernel(parts_ref, packed_ref):
    gram = real_form(*unpack(jnp.sum(parts_ref[...], 0)))
    rows = lax.broadcasted_iota(jnp.int32, (COLS, COLS), 0)
    cols = lax.broadcasted_iota(jnp.int32, (COLS, COLS), 1)
    ident = (rows == cols).astype(jnp.float32)
    trace = jnp.sum(gram * ident)
    inner = gram / trace
    factor = 1.5 * ident - 0.5 * inner
    mapping = factor / jnp.sqrt(trace)
    for sweep in range(NS_STEPS - 1):
        right = right_of(factor)
        half = product(left_of(inner), right)
        inner = product(left_of(half), right)
        factor = 1.5 * ident - 0.5 * inner
        mapping = product(left_of(mapping), right_of(factor))
    packed = pack(mapping[:HALF, :HALF], mapping[:HALF, HALF:])
    packed_ref[...] = jnp.broadcast_to(packed[None], packed_ref.shape)


def apply_kernel(packed_ref, spectra_ref, shapes_ref):
    for spot in range(spectra_ref.shape[0]):
        mapping = real_form(*unpack(packed_ref[spot])).astype(jnp.bfloat16)
        rows = spectra_ref[spot].reshape(-1, COLS)
        shapes = jnp.dot(rows, mapping, preferred_element_type=jnp.float32)
        shapes_ref[spot] = shapes.astype(jnp.bfloat16).reshape(shapes_ref.shape[1:])


def local(spectra, weights):
    freq_count, var_count, point_count, col_count = spectra.shape
    step = 2
    block = pl.BlockSpec((step, var_count, point_count, col_count), lambda f: (f, 0, 0, 0))
    small = pl.BlockSpec((step, HALF // 2, COLS), lambda f: (f, 0, 0))
    packed_shape = jax.ShapeDtypeStruct((freq_count, HALF // 2, COLS), jnp.float32)
    packed = pl.pallas_call(
        gram_kernel,
        grid=(freq_count // step,),
        in_specs=[block, pl.BlockSpec((point_count // COLS, COLS), lambda f: (0, 0))],
        out_specs=small,
        out_shape=packed_shape,
        scratch_shapes=[pltpu.VMEM((point_count, COLS), jnp.float32)],
    )(spectra, weights.reshape(point_count // COLS, COLS))
    parts = lax.all_to_all(packed, "pts", 0, 0, tiled=True)
    own = pl.pallas_call(
        polar_kernel,
        in_specs=[pl.BlockSpec(memory_space=pltpu.VMEM)],
        out_specs=pl.BlockSpec(memory_space=pltpu.VMEM),
        out_shape=packed_shape,
    )(parts)
    mappings = lax.all_to_all(own, "pts", 0, 0, tiled=True)
    return pl.pallas_call(
        apply_kernel,
        grid=(freq_count // step,),
        in_specs=[small, block],
        out_specs=block,
        out_shape=jax.ShapeDtypeStruct(spectra.shape, jnp.bfloat16),
    )(mappings, spectra)


def solution(mesh):
    in_specs = (P("freq", None, "pts", None), P("pts"))
    out_specs = P("freq", None, "pts", None)
    return jax.shard_map(local, mesh=mesh, in_specs=in_specs, out_specs=out_specs, check_vma=False)
```

time: 950 us -> 52.6 us (0.06); the launches traced: 936 us -> 52 us
  other arithmetic: 655 us -> 0 us
  matrix products: 160 us -> 0 us
  waiting for transfers between devices: 90.1 us -> 0 us
  blocking collectives: 0 us -> 29.8 us
  Pallas kernels: 0 us -> 22.1 us
  between operations: 13.8 us -> 0.01 us
  local copies, waits for them, and re-layouts: 9.6 us -> 0 us
    add x256 -> x0, other arithmetic: 365 us -> none  [the longest x128 340 us: eliminate(): factor = factor + scaled[:, None, :] * picker[None, :, None]]
    reduce_sum x513 -> x0, other arithmetic: 263 us -> none  [the longest x128 200 us: eliminate(): current = jnp.sum(working * picker[None, None, :], axis=2) * below[None, :]]
    dot_general x150 -> x0, matrix products: 160 us -> none  [the longest x128 120 us: back_step(): jnp.einsum('fj,fjk->fk', factor_row, solved, precision=lax.Precision.HIGH...]
    psum x1 -> x0, waiting for transfers between devices: 90.1 us -> none  [local(): summed = lax.psum(cross_gram, 'pts')]
    all_to_all x0 -> x2, blocking collectives: none -> 29.8 us  [the longest x1 17 us: local(): parts = lax.all_to_all(packed, 'pts', 0, 0, tiled=True)]
    pallas_call x0 -> x3, Pallas kernels: none -> 22.1 us  [the longest x1 8.83 us: local(): pl.pallas_call(apply_kernel, grid=(freq_count // step,), in_specs=[small,...]
    div x256 -> x0, other arithmetic: 20.1 us -> none  [the longest x128 10.1 us: eliminate(): scaled = current / pivot[:, None]]
  transfers between devices with their start and end apart: 1 -> 0, of which waited for: 1 -> 0; matrix products, arithmetic and copies ran while one was open for 0% -> 0% of each run, Pallas kernels for 0% -> 0%
where the time goes in v1:
time: 52.6 us; the launch traced here: 52 us
  blocking collectives  29.8 us (57%)
  Pallas kernels  22.1 us (42%)
    all_to_all x1, blocking collectives, local(): parts = lax.all_to_all(packed, 'pts', 0, 0, tiled=True)  17 us
    all_to_all x1, blocking collectives, local(): mappings = lax.all_to_all(own, 'pts', 0, 0, tiled=True)  12.9 us
    pallas_call x1, Pallas kernels, local(): pl.pallas_call(apply_kernel, grid=(freq_count // step,), in_specs=[small,...  8.83 us
    pallas_call x1, Pallas kernels, local(): pl.pallas_call(gram_kernel, grid=(freq_count // step,), in_specs=[block,...  8.24 us
    pallas_call x1, Pallas kernels, local(): pl.pallas_call(polar_kernel, in_specs=[pl.BlockSpec(memory_space=pltpu.VM...  5.07 us

profile of v1, /device:TPU:0, one launch (start us, length us, event | category | flops | bytes accessed | tf_op | source)
XLA Modules:
  0.0 52.0 jit_solution(16183601738077531744)
XLA Ops:
  0.0 8.2 %shard_map.28 = f32[16,32,128]{2,1,0:T(8,128)} custom-call(bf16[16,5,256,128]{3,2,1,0:T(8,128)(2,1)} %spectra_ref.3, f32[2,128]{1,0:T(2,128)} %bitcast.1), custom_call_target="tpu_custom_call" | custom-call | tf_op jit(solution)/shard_map/pallas_call | solution.py:111
  8.2 17.0 %all_to_all.10.parts_ref = f32[16,32,128]{2,1,0:T(8,128)} all-to-all(f32[16,32,128]{2,1,0:T(8,128)} %shard_map.28), channel_id=1, replica_groups=mesh['pts'=16,'freq'=8] {'pts'}, dimensions={0} | all-to-all | bytes 524288 | tf_op jit(solution)/shard_map/all_to_all | solution.py:119
  25.2 5.1 %shard_map.29 = f32[16,32,128]{2,1,0:T(8,128)} custom-call(f32[16,32,128]{2,1,0:T(8,128)} %all_to_all.10.parts_ref), custom_call_target="tpu_custom_call" | custom-call | tf_op jit(solution)/shard_map/pallas_call | solution.py:120
  30.3 12.9 %all_to_all.11.packed_ref = f32[16,32,128]{2,1,0:T(8,128)} all-to-all(f32[16,32,128]{2,1,0:T(8,128)} %shard_map.29), channel_id=1, replica_groups=mesh['pts'=16,'freq'=8] {'pts'}, dimensions={0} | all-to-all | bytes 524288 | tf_op jit(solution)/shard_map/all_to_all | solution.py:126
  43.2 8.8 %shard_map.30 = bf16[16,5,256,128]{3,2,1,0:T(8,128)(2,1)} custom-call(f32[16,32,128]{2,1,0:T(8,128)} %all_to_all.11.packed_ref, bf16[16,5,256,128]{3,2,1,0:T(8,128)(2,1)} %spectra_ref.3), custom_call_target="tpu_custom_call" | custom-call | tf_op jit(solution)/shard_map/pallas_call | solution.py:127

commit v2 on v1

--- a/solution.py
+++ b/solution.py
@@ -37,22 +37,36 @@
     return jnp.concatenate([upper_row, lower_row], 0)
 
 
-def gram_kernel(spectra_ref, weights_ref, packed_ref, root_ref):
-    @pl.when(pl.program_id(0) == 0)
-    def _():
-        for part in range(weights_ref.shape[0]):
-            row = jnp.sqrt(weights_ref[part : part + 1, :])
-            root_ref[part * COLS : (part + 1) * COLS, :] = jnp.broadcast_to(row, (COLS, COLS)).T
+def gram_kernel(spectra_ref, weights_ref, packed_ref, held_ref, near_ref, root_ref, near_sem, sems):
+    freq_count = spectra_ref.shape[0]
+    step = freq_count // sems.shape[0]
 
-    for spot in range(spectra_ref.shape[0]):
-        weighted = (root_ref[...][None] * spectra_ref[spot].astype(jnp.float32)).astype(jnp.bfloat16)
-        rows = weighted.reshape(-1, COLS)
-        products = lax.dot_general(
-            rows, rows, (((0,), (0,)), ((), ())), preferred_element_type=jnp.float32
-        )
-        real_part = products[:HALF, :HALF] + products[HALF:, HALF:]
-        imag_part = products[:HALF, HALF:] - products[HALF:, :HALF]
-        packed_ref[spot] = pack(real_part, imag_part)
+    def load(spot):
+        place = pl.ds(spot * step, step)
+        return pltpu.make_async_copy(spectra_ref.at[place], held_ref.at[place], sems.at[spot])
+
+    near = pltpu.make_async_copy(weights_ref, near_ref, near_sem)
+    near.start()
+    for spot in range(sems.shape[0]):
+        load(spot).start()
+    near.wait()
+    for part in range(near_ref.shape[0]):
+        row = jnp.sqrt(near_ref[part : part + 1, :])
+        root_ref[part * COLS : (part + 1) * COLS, :] = jnp.broadcast_to(row, (COLS, COLS)).T
+
+    @pl.loop(0, sems.shape[0])
+    def _(spot):
+        load(spot).wait()
+        for inside in range(step):
+            freq = spot * step + inside
+            weighted = (root_ref[...][None] * held_ref[freq].astype(jnp.float32)).astype(jnp.bfloat16)
+            rows = weighted.reshape(-1, COLS)
+            products = lax.dot_general(
+                rows, rows, (((0,), (0,)), ((), ())), preferred_element_type=jnp.float32
+            )
+            real_part = products[:HALF, :HALF] + products[HALF:, HALF:]
+            imag_part = products[:HALF, HALF:] - products[HALF:, :HALF]
+            packed_ref[freq] = pack(real_part, imag_part)
 
 
 def split(value):
@@ -94,43 +108,77 @@
     packed_ref[...] = jnp.broadcast_to(packed[None], packed_ref.shape)
 
 
-def apply_kernel(packed_ref, spectra_ref, shapes_ref):
-    for spot in range(spectra_ref.shape[0]):
-        mapping = real_form(*unpack(packed_ref[spot])).astype(jnp.bfloat16)
-        rows = spectra_ref[spot].reshape(-1, COLS)
-        shapes = jnp.dot(rows, mapping, preferred_element_type=jnp.float32)
-        shapes_ref[spot] = shapes.astype(jnp.bfloat16).reshape(shapes_ref.shape[1:])
+def apply_kernel(packed_ref, spectra_ref, shapes_ref, staged_ref, sems):
+    freq_count = spectra_ref.shape[0]
+    step = freq_count // sems.shape[0]
+
+    def save(spot):
+        place = pl.ds(spot * step, step)
+        return pltpu.make_async_copy(staged_ref.at[place], shapes_ref.at[place], sems.at[spot])
+
+    @pl.loop(0, sems.shape[0])
+    def _(spot):
+        for inside in range(step):
+            freq = spot * step + inside
+            mapping = real_form(*unpack(packed_ref[freq])).astype(jnp.bfloat16)
+            rows = spectra_ref[freq].reshape(-1, COLS)
+            shapes = jnp.dot(rows, mapping, preferred_element_type=jnp.float32)
+            staged_ref[freq] = shapes.astype(jnp.bfloat16).reshape(staged_ref.shape[1:])
+        save(spot).start()
+
+    for spot in range(sems.shape[0]):
+        save(spot).wait()
+
+
+LOADS = 2
+SAVES = 2
+MIB = 1 << 20
 
 
 def local(spectra, weights):
     freq_count, var_count, point_count, col_count = spectra.shape
-    step = 2
-    block = pl.BlockSpec((step, var_count, point_count, col_count), lambda f: (f, 0, 0, 0))
-    small = pl.BlockSpec((step, HALF // 2, COLS), lambda f: (f, 0, 0))
-    packed_shape = jax.ShapeDtypeStruct((freq_count, HALF // 2, COLS), jnp.float32)
-    packed = pl.pallas_call(
+    hbm = pl.BlockSpec(memory_space=pltpu.HBM)
+    vmem = pl.BlockSpec(memory_space=pltpu.VMEM)
+    packed_shape = (freq_count, HALF // 2, COLS)
+    packed, held = pl.pallas_call(
         gram_kernel,
-        grid=(freq_count // step,),
-        in_specs=[block, pl.BlockSpec((point_count // COLS, COLS), lambda f: (0, 0))],
-        out_specs=small,
-        out_shape=packed_shape,
-        scratch_shapes=[pltpu.VMEM((point_count, COLS), jnp.float32)],
-    )(spectra, weights.reshape(point_count // COLS, COLS))
+        in_specs=[hbm, hbm],
+        out_specs=[vmem, vmem],
+        out_shape=[pltpu.VMEM(packed_shape, jnp.float32), pltpu.VMEM(spectra.shape, spectra.dtype)],
+        scratch_shapes=[
+            pltpu.VMEM((point_count // COLS, COLS), jnp.float32),
+            pltpu.VMEM((point_count, COLS), jnp.float32),
+            pltpu.SemaphoreType.DMA,
+            pltpu.SemaphoreType.DMA((LOADS,)),
+        ],
+        compiler_params=pltpu.CompilerParams(vmem_limit_bytes=8 * MIB),
+        name="gram",
+    )(
+        pltpu.with_memory_space_constraint(spectra, pltpu.HBM),
+        pltpu.with_memory_space_constraint(weights.reshape(point_count // COLS, COLS), pltpu.HBM),
+    )
     parts = lax.all_to_all(packed, "pts", 0, 0, tiled=True)
     own = pl.pallas_call(
         polar_kernel,
-        in_specs=[pl.BlockSpec(memory_space=pltpu.VMEM)],
-        out_specs=pl.BlockSpec(memory_space=pltpu.VMEM),
-        out_shape=packed_shape,
-    )(parts)
+        in_specs=[vmem],
+        out_specs=vmem,
+        out_shape=pltpu.VMEM(packed_shape, jnp.float32),
+        compiler_params=pltpu.CompilerParams(vmem_limit_bytes=8 * MIB),
+        name="polar",
+    )(pltpu.with_memory_space_constraint(parts, pltpu.VMEM))
     mappings = lax.all_to_all(own, "pts", 0, 0, tiled=True)
     return pl.pallas_call(
         apply_kernel,
-        grid=(freq_count // step,),
-        in_specs=[small, block],
-        out_specs=block,
+        in_specs=[vmem, vmem],
+        out_specs=hbm,
         out_shape=jax.ShapeDtypeStruct(spectra.shape, jnp.bfloat16),
-    )(mappings, spectra)
+        scratch_shapes=[
+            pltpu.VMEM(spectra.shape, jnp.bfloat16),
+            pltpu.SemaphoreType.DMA((SAVES,)),
+        ],
+        compiler_params=pltpu.CompilerParams(vmem_limit_bytes=16 * MIB),
+        name="apply",
+    )(pltpu.with_memory_space_constraint(mappings, pltpu.VMEM), held)
 
 
 def solution(mesh):

time: 52.6 us -> 41 us (0.78)
  Pallas kernels: 22.1 us -> 12.5 us
  blocking collectives: 29.8 us -> 28.2 us
    pallas_call x3, Pallas kernels: 22.1 us -> 12.5 us  [the longest x1 5.52 us: local(): pl.pallas_call(gram_kernel, in_specs=[hbm, hbm], out_specs=[vmem, vmem],...]
    all_to_all x1, blocking collectives: 12.9 us -> 11.6 us  [local(): mappings = lax.all_to_all(own, 'pts', 0, 0, tiled=True)]
where the time goes in v2:
time: 41 us; the launch traced here: 40.8 us
  blocking collectives  28.2 us (69%)
  Pallas kernels  12.5 us (30%)
    all_to_all x1, blocking collectives, local(): parts = lax.all_to_all(packed, 'pts', 0, 0, tiled=True)  16.7 us
    all_to_all x1, blocking collectives, local(): mappings = lax.all_to_all(own, 'pts', 0, 0, tiled=True)  11.6 us
    pallas_call x1, Pallas kernels, local(): pl.pallas_call(gram_kernel, in_specs=[hbm, hbm], out_specs=[vmem, vmem],...  5.52 us
    pallas_call x1, Pallas kernels, local(): pl.pallas_call(apply_kernel, in_specs=[vmem, vmem], out_specs=hbm, out_sh...  3.59 us
    pallas_call x1, Pallas kernels, local(): pl.pallas_call(polar_kernel, in_specs=[vmem], out_specs=vmem, out_shape=p...  3.41 us

profile of v2, /device:TPU:0, one launch (start us, length us, event | category | flops | bytes accessed | tf_op | source)
XLA Modules:
  0.0 40.8 jit_solution(6900367603839107011)
XLA Ops:
  0.0 5.5 %gram.1 = (f32[16,32,128]{2,1,0:T(8,128)S(1)}, bf16[16,5,256,128]{3,2,1,0:T(8,128)(2,1)S(1)}) custom-call(bf16[16,5,256,128]{3,2,1,0:T(8,128)(2,1)} %spectra_ref.1, f32[2,128]{1,0:T(2,128)} %bitcast.1), custom_call_target="tpu_custom_call" | custom-call | tf_op jit(solution)/shard_map/gram/pallas_call | solution.py:143
  5.5 16.7 %all_to_all.10.parts_ref = f32[16,32,128]{2,1,0:T(8,128)S(1)} all-to-all(f32[16,32,128]{2,1,0:T(8,128)S(1)} %get-tuple-element.7), channel_id=1, replica_groups=mesh['pts'=16,'freq'=8] {'pts'}, dimensions={0} | all-to-all | bytes 524288 | tf_op jit(solution)/shard_map/all_to_all | solution.py:160
  22.2 3.4 %polar.1 = f32[16,32,128]{2,1,0:T(8,128)S(1)} custom-call(f32[16,32,128]{2,1,0:T(8,128)S(1)} %all_to_all.10.parts_ref), custom_call_target="tpu_custom_call" | custom-call | tf_op jit(solution)/shard_map/polar/pallas_call | solution.py:161
  25.6 11.6 %all_to_all.11.packed_ref = f32[16,32,128]{2,1,0:T(8,128)S(1)} all-to-all(f32[16,32,128]{2,1,0:T(8,128)S(1)} %polar.1), channel_id=1, replica_groups=mesh['pts'=16,'freq'=8] {'pts'}, dimensions={0} | all-to-all | bytes 524288 | tf_op jit(solution)/shard_map/all_to_all | solution.py:169
  37.2 3.6 %apply.1 = bf16[16,5,256,128]{3,2,1,0:T(8,128)(2,1)} custom-call(f32[16,32,128]{2,1,0:T(8,128)S(1)} %all_to_all.11.packed_ref, bf16[16,5,256,128]{3,2,1,0:T(8,128)(2,1)S(1)} %get-tuple-element.8.spectra_ref), custom_call_target="tpu_custom_call" | custom-call | tf_op jit(solution)/shard_map/apply/pallas_call | solution.py:170

commit v3 on v2

v3 whole, which is shorter than its diff:
```python
import jax
import jax.numpy as jnp
from jax import lax
from jax.experimental import pallas as pl
from jax.experimental.pallas import tpu as pltpu
from jax.sharding import PartitionSpec as P

NS_STEPS = 10
HALF = 64
COLS = 2 * HALF


def places(rows):
    row = lax.broadcasted_iota(jnp.int32, (rows, COLS), 0)
    col = lax.broadcasted_iota(jnp.int32, (rows, COLS), 1)
    return row % HALF, col % HALF, row < HALF, col < HALF


def pack(square):
    row, col, _, left = places(HALF)
    top, bottom = square[:HALF], square[HALF:]
    lower = row >= col
    chosen = jnp.where(left == lower, top, jnp.where(left, -bottom, bottom))
    upper_rows, lower_rows = chosen[: HALF // 2], chosen[HALF // 2 :]
    left = left[: HALF // 2]
    keep = jnp.where(left, upper_rows, lower_rows)
    move = jnp.where(left, lower_rows, upper_rows)
    return keep + pltpu.roll(move, HALF, 1)


def unpack(packed):
    row, col, above, left = places(COLS)
    turned = pltpu.roll(packed, HALF, 1)
    half_left = left[: HALF // 2]
    upper_rows = jnp.where(half_left, packed, turned)
    lower_rows = jnp.where(half_left, turned, packed)
    tiled = jnp.concatenate([upper_rows, lower_rows, upper_rows, lower_rows], 0)
    flipped = tiled.T
    real_part = jnp.where(row >= col, tiled, flipped)
    imag_part = jnp.where(row < col, tiled, jnp.where(row > col, -flipped, 0.0))
    return jnp.where(above == left, real_part, jnp.where(above, imag_part, -imag_part))


def gram_kernel(spectra_ref, weights_ref, packed_ref, held_ref, near_ref, root_ref, near_sem, sems):
    near = pltpu.make_async_copy(weights_ref, near_ref, near_sem)
    near.start()
    loads = []
    first = 0
    for spot, step in enumerate(LOADS):
        place = pl.ds(first, step)
        loads.append(pltpu.make_async_copy(spectra_ref.at[place], held_ref.at[place], sems.at[spot]))
        loads[-1].start()
        first += step
    near.wait()
    for part in range(near_ref.shape[0]):
        row = jnp.sqrt(near_ref[part : part + 1, :])
        root_ref[part * COLS : (part + 1) * COLS, :] = jnp.broadcast_to(row, (COLS, COLS)).T

    first = 0
    for spot, step in enumerate(LOADS):
        loads[spot].wait()
        for freq in range(first, first + step):
            weighted = (root_ref[...][None] * held_ref[freq].astype(jnp.float32)).astype(jnp.bfloat16)
            rows = weighted.reshape(-1, COLS)
            products = lax.dot_general(
                rows, rows, (((0,), (0,)), ((), ())), preferred_element_type=jnp.float32
            )
            packed_ref[freq] = pack(products)
        first += step


def split(value):
    high = value.astype(jnp.bfloat16)
    low = (value - high.astype(jnp.float32)).astype(jnp.bfloat16)
    return high, low


def left_of(value):
    return jnp.concatenate(split(value), 1)


def right_of(value):
    row = jnp.concatenate(split(value), 1)
    return jnp.concatenate([row, row], 0)


def product(left, right):
    both = jnp.dot(left, right, preferred_element_type=jnp.float32)
    return both[:, :COLS] + both[:, COLS:]


def polar_kernel(parts_ref, packed_ref):
    gram = unpack(jnp.sum(parts_ref[...], 0))
    rows = lax.broadcasted_iota(jnp.int32, (COLS, COLS), 0)
    cols = lax.broadcasted_iota(jnp.int32, (COLS, COLS), 1)
    ident = (rows == cols).astype(jnp.float32)
    trace = jnp.sum(gram * ident)
    inner = gram / trace
    factor = 1.5 * ident - 0.5 * inner
    mapping = factor / jnp.sqrt(trace)
    for sweep in range(NS_STEPS - 1):
        right = right_of(factor)
        half = product(left_of(inner), right)
        inner = product(left_of(half), right)
        if sweep > 0:
            mapping = product(left_of(mapping), right)
        factor = 1.5 * ident - 0.5 * inner
    mapping = product(left_of(mapping), right_of(factor))
    packed = 0.5 * pack(mapping)
    packed_ref[...] = jnp.broadcast_to(packed[None], packed_ref.shape)


def apply_kernel(packed_ref, spectra_ref, shapes_ref, staged_ref, sems):
    saves = []
    first = 0
    for spot, step in enumerate(SAVES):
        for freq in range(first, first + step, 2):
            pair = [unpack(packed_ref[freq + k]).astype(jnp.bfloat16) for k in range(2)]
            blank = jnp.zeros_like(pair[0])
            mapping = jnp.concatenate(
                [jnp.concatenate([pair[0], blank], 1), jnp.concatenate([blank, pair[1]], 1)], 0
            )
            rows = jnp.concatenate([spectra_ref[freq + k].reshape(-1, COLS) for k in range(2)], 1)
            shapes = jnp.dot(rows, mapping, preferred_element_type=jnp.float32).astype(jnp.bfloat16)
            for k in range(2):
                part = shapes[:, k * COLS : (k + 1) * COLS]
                staged_ref[freq + k] = part.reshape(staged_ref.shape[1:])
        place = pl.ds(first, step)
        saves.append(pltpu.make_async_copy(staged_ref.at[place], shapes_ref.at[place], sems.at[spot]))
        saves[-1].start()
        first += step
    for save in saves:
        save.wait()


LOADS = (6, 10)
SAVES = (4, 4, 4, 4)
MIB = 1 << 20


def local(spectra, weights):
    freq_count, var_count, point_count, col_count = spectra.shape
    hbm = pl.BlockSpec(memory_space=pltpu.HBM)
    vmem = pl.BlockSpec(memory_space=pltpu.VMEM)
    packed_shape = (freq_count, HALF // 2, COLS)
    packed, held = pl.pallas_call(
        gram_kernel,
        in_specs=[hbm, hbm],
        out_specs=[vmem, vmem],
        out_shape=[pltpu.VMEM(packed_shape, jnp.float32), pltpu.VMEM(spectra.shape, spectra.dtype)],
        scratch_shapes=[
            pltpu.VMEM((point_count // COLS, COLS), jnp.float32),
            pltpu.VMEM((point_count, COLS), jnp.float32),
            pltpu.SemaphoreType.DMA,
            pltpu.SemaphoreType.DMA((len(LOADS),)),
        ],
        compiler_params=pltpu.CompilerParams(vmem_limit_bytes=8 * MIB),
        name="gram",
    )(
        pltpu.with_memory_space_constraint(spectra, pltpu.HBM),
        pltpu.with_memory_space_constraint(weights.reshape(point_count // COLS, COLS), pltpu.HBM),
    )
    parts = lax.all_to_all(packed, "pts", 0, 0, tiled=True)
    own = pl.pallas_call(
        polar_kernel,
        in_specs=[vmem],
        out_specs=vmem,
        out_shape=pltpu.VMEM(packed_shape, jnp.float32),
        compiler_params=pltpu.CompilerParams(vmem_limit_bytes=8 * MIB),
        name="polar",
    )(pltpu.with_memory_space_constraint(parts, pltpu.VMEM))
    mappings = lax.all_to_all(own, "pts", 0, 0, tiled=True)
    return pl.pallas_call(
        apply_kernel,
        in_specs=[vmem, vmem],
        out_specs=hbm,
        out_shape=jax.ShapeDtypeStruct(spectra.shape, jnp.bfloat16),
        scratch_shapes=[
            pltpu.VMEM(spectra.shape, jnp.bfloat16),
            pltpu.SemaphoreType.DMA((len(SAVES),)),
        ],
        compiler_params=pltpu.CompilerParams(vmem_limit_bytes=16 * MIB),
        name="apply",
    )(pltpu.with_memory_space_constraint(mappings, pltpu.VMEM), held)


def solution(mesh):
    in_specs = (P("freq", None, "pts", None), P("pts"))
    out_specs = P("freq", None, "pts", None)
    return jax.shard_map(local, mesh=mesh, in_specs=in_specs, out_specs=out_specs, check_vma=False)
```

time: 41 us -> 38.5 us (0.939)
  Pallas kernels: 12.5 us -> 10.1 us
    pallas_call x1, Pallas kernels: 5.52 us -> 3.71 us  [local(): pl.pallas_call(gram_kernel, in_specs=[hbm, hbm], out_specs=[vmem, vmem],...]
    pallas_call x1, Pallas kernels: 3.59 us -> 3.08 us  [local(): pl.pallas_call(apply_kernel, in_specs=[vmem, vmem], out_specs=hbm, out_sh...]
where the time goes in v3:
time: 38.5 us; the launch traced here: 38.3 us
  blocking collectives  28.2 us (73%)
  Pallas kernels  10.1 us (26%)
    all_to_all x1, blocking collectives, local(): parts = lax.all_to_all(packed, 'pts', 0, 0, tiled=True)  16.7 us
    all_to_all x1, blocking collectives, local(): mappings = lax.all_to_all(own, 'pts', 0, 0, tiled=True)  11.6 us
    pallas_call x1, Pallas kernels, local(): pl.pallas_call(gram_kernel, in_specs=[hbm, hbm], out_specs=[vmem, vmem],...  3.71 us
    pallas_call x1, Pallas kernels, local(): pl.pallas_call(polar_kernel, in_specs=[vmem], out_specs=vmem, out_shape=p...  3.27 us
    pallas_call x1, Pallas kernels, local(): pl.pallas_call(apply_kernel, in_specs=[vmem, vmem], out_specs=hbm, out_sh...  3.08 us

profile of v3, /device:TPU:0, one launch (start us, length us, event | category | flops | bytes accessed | tf_op | source)
XLA Modules:
  0.0 38.3 jit_solution(12548818650279402294)
XLA Ops:
  0.0 3.7 %gram.1 = (f32[16,32,128]{2,1,0:T(8,128)S(1)}, bf16[16,5,256,128]{3,2,1,0:T(8,128)(2,1)S(1)}) custom-call(bf16[16,5,256,128]{3,2,1,0:T(8,128)(2,1)} %spectra_ref.1, f32[2,128]{1,0:T(2,128)} %bitcast.1), custom_call_target="tpu_custom_call" | custom-call | tf_op jit(solution)/shard_map/gram/pallas_call | solution.py:146
  3.7 16.7 %all_to_all.10.parts_ref = f32[16,32,128]{2,1,0:T(8,128)S(1)} all-to-all(f32[16,32,128]{2,1,0:T(8,128)S(1)} %get-tuple-element.7), channel_id=1, replica_groups=mesh['pts'=16,'freq'=8] {'pts'}, dimensions={0} | all-to-all | bytes 524288 | tf_op jit(solution)/shard_map/all_to_all | solution.py:163
  20.4 3.3 %polar.1 = f32[16,32,128]{2,1,0:T(8,128)S(1)} custom-call(f32[16,32,128]{2,1,0:T(8,128)S(1)} %all_to_all.10.parts_ref), custom_call_target="tpu_custom_call" | custom-call | tf_op jit(solution)/shard_map/polar/pallas_call | solution.py:164
  23.6 11.6 %all_to_all.11.packed_ref = f32[16,32,128]{2,1,0:T(8,128)S(1)} all-to-all(f32[16,32,128]{2,1,0:T(8,128)S(1)} %polar.1), channel_id=1, replica_groups=mesh['pts'=16,'freq'=8] {'pts'}, dimensions={0} | all-to-all | bytes 524288 | tf_op jit(solution)/shard_map/all_to_all | solution.py:172
  35.2 3.1 %apply.1 = bf16[16,5,256,128]{3,2,1,0:T(8,128)(2,1)} custom-call(f32[16,32,128]{2,1,0:T(8,128)S(1)} %all_to_all.11.packed_ref, bf16[16,5,256,128]{3,2,1,0:T(8,128)(2,1)S(1)} %get-tuple-element.8.spectra_ref), custom_call_target="tpu_custom_call" | custom-call | tf_op jit(solution)/shard_map/apply/pallas_call | solution.py:173

commit v4 on v3

--- a/solution.py
+++ b/solution.py
@@ -49,7 +49,7 @@
     for spot, step in enumerate(LOADS):
         place = pl.ds(first, step)
         loads.append(pltpu.make_async_copy(spectra_ref.at[place], held_ref.at[place], sems.at[spot]))
-        loads[-1].start()
+        loads[-1].start(priority=min(spot, 1))
         first += step
     near.wait()
     for part in range(near_ref.shape[0]):
@@ -90,14 +90,17 @@
 
 
 def polar_kernel(parts_ref, packed_ref):
-    gram = unpack(jnp.sum(parts_ref[...], 0))
+    packed = jnp.sum(parts_ref[...], 0)
+    gram = unpack(packed)
+    row, col, _, left = places(HALF // 2)
+    diagonal = jnp.where(left, row, row + HALF // 2) == col
+    trace = 2.0 * jnp.sum(jnp.where(diagonal, packed, 0.0), keepdims=True)
     rows = lax.broadcasted_iota(jnp.int32, (COLS, COLS), 0)
     cols = lax.broadcasted_iota(jnp.int32, (COLS, COLS), 1)
     ident = (rows == cols).astype(jnp.float32)
-    trace = jnp.sum(gram * ident)
-    inner = gram / trace
+    inner = gram * (1.0 / trace)
     factor = 1.5 * ident - 0.5 * inner
-    mapping = factor / jnp.sqrt(trace)
+    mapping = factor * (1.0 / jnp.sqrt(trace))
     for sweep in range(NS_STEPS - 1):
         right = right_of(factor)
         half = product(left_of(inner), right)
@@ -133,7 +136,7 @@
         save.wait()
 
 
-LOADS = (6, 10)
+LOADS = (4, 6, 6)
 SAVES = (4, 4, 4, 4)
 MIB = 1 << 20
 

time: 38.5 us -> 38.3 us (level)
  no operation moved by 1% of the time
where the time goes in v4:
time: 38.3 us; the launch traced here: 38.1 us
  blocking collectives  28.2 us (74%)
  Pallas kernels  9.81 us (26%)
    all_to_all x1, blocking collectives, local(): parts = lax.all_to_all(packed, 'pts', 0, 0, tiled=True)  16.7 us
    all_to_all x1, blocking collectives, local(): mappings = lax.all_to_all(own, 'pts', 0, 0, tiled=True)  11.6 us
    pallas_call x1, Pallas kernels, local(): pl.pallas_call(gram_kernel, in_specs=[hbm, hbm], out_specs=[vmem, vmem],...  3.58 us
    pallas_call x1, Pallas kernels, local(): pl.pallas_call(polar_kernel, in_specs=[vmem], out_specs=vmem, out_shape=p...  3.14 us
    pallas_call x1, Pallas kernels, local(): pl.pallas_call(apply_kernel, in_specs=[vmem, vmem], out_specs=hbm, out_sh...  3.08 us

profile of v4, /device:TPU:0, one launch (start us, length us, event | category | flops | bytes accessed | tf_op | source)
XLA Modules:
  0.0 38.1 jit_solution(14602419542961581986)
XLA Ops:
  0.0 3.6 %gram.1 = (f32[16,32,128]{2,1,0:T(8,128)S(1)}, bf16[16,5,256,128]{3,2,1,0:T(8,128)(2,1)S(1)}) custom-call(bf16[16,5,256,128]{3,2,1,0:T(8,128)(2,1)} %spectra_ref.1, f32[2,128]{1,0:T(2,128)} %bitcast.1), custom_call_target="tpu_custom_call" | custom-call | tf_op jit(solution)/shard_map/gram/pallas_call | solution.py:149
  3.6 16.7 %all_to_all.10.parts_ref = f32[16,32,128]{2,1,0:T(8,128)S(1)} all-to-all(f32[16,32,128]{2,1,0:T(8,128)S(1)} %get-tuple-element.7), channel_id=1, replica_groups=mesh['pts'=16,'freq'=8] {'pts'}, dimensions={0} | all-to-all | bytes 524288 | tf_op jit(solution)/shard_map/all_to_all | solution.py:166
  20.2 3.1 %polar.1 = f32[16,32,128]{2,1,0:T(8,128)S(1)} custom-call(f32[16,32,128]{2,1,0:T(8,128)S(1)} %all_to_all.10.parts_ref), custom_call_target="tpu_custom_call" | custom-call | tf_op jit(solution)/shard_map/polar/pallas_call | solution.py:167
  23.4 11.6 %all_to_all.11.packed_ref = f32[16,32,128]{2,1,0:T(8,128)S(1)} all-to-all(f32[16,32,128]{2,1,0:T(8,128)S(1)} %polar.1), channel_id=1, replica_groups=mesh['pts'=16,'freq'=8] {'pts'}, dimensions={0} | all-to-all | bytes 524288 | tf_op jit(solution)/shard_map/all_to_all | solution.py:175
  35.0 3.1 %apply.1 = bf16[16,5,256,128]{3,2,1,0:T(8,128)(2,1)} custom-call(f32[16,32,128]{2,1,0:T(8,128)S(1)} %all_to_all.11.packed_ref, bf16[16,5,256,128]{3,2,1,0:T(8,128)(2,1)S(1)} %get-tuple-element.8.spectra_ref), custom_call_target="tpu_custom_call" | custom-call | tf_op jit(solution)/shard_map/apply/pallas_call | solution.py:176

commit v5 on v4

--- a/solution.py
+++ b/solution.py
@@ -100,7 +100,7 @@
     ident = (rows == cols).astype(jnp.float32)
     inner = gram * (1.0 / trace)
     factor = 1.5 * ident - 0.5 * inner
-    mapping = factor * (1.0 / jnp.sqrt(trace))
+    mapping = factor[:HALF] * (1.0 / jnp.sqrt(trace))
     for sweep in range(NS_STEPS - 1):
         right = right_of(factor)
         half = product(left_of(inner), right)
@@ -109,8 +109,9 @@
             mapping = product(left_of(mapping), right)
         factor = 1.5 * ident - 0.5 * inner
     mapping = product(left_of(mapping), right_of(factor))
-    packed = 0.5 * pack(mapping)
-    packed_ref[...] = jnp.broadcast_to(packed[None], packed_ref.shape)
+    packed = pack(jnp.concatenate([mapping, jnp.zeros_like(mapping)], 0))
+    for spot in range(packed_ref.shape[0]):
+        packed_ref[spot] = packed
 
 
 def apply_kernel(packed_ref, spectra_ref, shapes_ref, staged_ref, sems):

time: 38.3 us -> 38.2 us (level)
  no operation moved by 1% of the time
where the time goes in v5:
time: 38.2 us; the launch traced here: 38.1 us
  blocking collectives  28.2 us (74%)
  Pallas kernels  9.79 us (26%)
    all_to_all x1, blocking collectives, local(): parts = lax.all_to_all(packed, 'pts', 0, 0, tiled=True)  16.7 us
    all_to_all x1, blocking collectives, local(): mappings = lax.all_to_all(own, 'pts', 0, 0, tiled=True)  11.6 us
    pallas_call x1, Pallas kernels, local(): pl.pallas_call(gram_kernel, in_specs=[hbm, hbm], out_specs=[vmem, vmem],...  3.58 us
    pallas_call x1, Pallas kernels, local(): pl.pallas_call(polar_kernel, in_specs=[vmem], out_specs=vmem, out_shape=p...  3.12 us
    pallas_call x1, Pallas kernels, local(): pl.pallas_call(apply_kernel, in_specs=[vmem, vmem], out_specs=hbm, out_sh...  3.08 us

profile of v5, /device:TPU:0, one launch (start us, length us, event | category | flops | bytes accessed | tf_op | source)
XLA Modules:
  0.0 38.1 jit_solution(11417577160194177050)
XLA Ops:
  0.0 3.6 %gram.1 = (f32[16,32,128]{2,1,0:T(8,128)S(1)}, bf16[16,5,256,128]{3,2,1,0:T(8,128)(2,1)S(1)}) custom-call(bf16[16,5,256,128]{3,2,1,0:T(8,128)(2,1)} %spectra_ref.1, f32[2,128]{1,0:T(2,128)} %bitcast.1), custom_call_target="tpu_custom_call" | custom-call | tf_op jit(solution)/shard_map/gram/pallas_call | solution.py:150
  3.6 16.7 %all_to_all.10.parts_ref = f32[16,32,128]{2,1,0:T(8,128)S(1)} all-to-all(f32[16,32,128]{2,1,0:T(8,128)S(1)} %get-tuple-element.7), channel_id=1, replica_groups=mesh['pts'=16,'freq'=8] {'pts'}, dimensions={0} | all-to-all | bytes 524288 | tf_op jit(solution)/shard_map/all_to_all | solution.py:167
  20.2 3.1 %polar.1 = f32[16,32,128]{2,1,0:T(8,128)S(1)} custom-call(f32[16,32,128]{2,1,0:T(8,128)S(1)} %all_to_all.10.parts_ref), custom_call_target="tpu_custom_call" | custom-call | tf_op jit(solution)/shard_map/polar/pallas_call | solution.py:168
  23.4 11.6 %all_to_all.11.packed_ref = f32[16,32,128]{2,1,0:T(8,128)S(1)} all-to-all(f32[16,32,128]{2,1,0:T(8,128)S(1)} %polar.1), channel_id=1, replica_groups=mesh['pts'=16,'freq'=8] {'pts'}, dimensions={0} | all-to-all | bytes 524288 | tf_op jit(solution)/shard_map/all_to_all | solution.py:176
  35.0 3.1 %apply.1 = bf16[16,5,256,128]{3,2,1,0:T(8,128)(2,1)} custom-call(f32[16,32,128]{2,1,0:T(8,128)S(1)} %all_to_all.11.packed_ref, bf16[16,5,256,128]{3,2,1,0:T(8,128)(2,1)S(1)} %get-tuple-element.8.spectra_ref), custom_call_target="tpu_custom_call" | custom-call | tf_op jit(solution)/shard_map/apply/pallas_call | solution.py:177

commit v6 on v5

--- a/solution.py
+++ b/solution.py
@@ -28,16 +28,16 @@
     return keep + pltpu.roll(move, HALF, 1)
 
 
-def unpack(packed):
+def unpack(packed, dtype):
     row, col, above, left = places(COLS)
     turned = pltpu.roll(packed, HALF, 1)
     half_left = left[: HALF // 2]
     upper_rows = jnp.where(half_left, packed, turned)
     lower_rows = jnp.where(half_left, turned, packed)
-    tiled = jnp.concatenate([upper_rows, lower_rows, upper_rows, lower_rows], 0)
+    tiled = jnp.concatenate([upper_rows, lower_rows, upper_rows, lower_rows], 0).astype(dtype)
     flipped = tiled.T
     real_part = jnp.where(row >= col, tiled, flipped)
-    imag_part = jnp.where(row < col, tiled, jnp.where(row > col, -flipped, 0.0))
+    imag_part = jnp.where(row < col, tiled, jnp.where(row > col, -flipped, jnp.zeros_like(tiled)))
     return jnp.where(above == left, real_part, jnp.where(above, imag_part, -imag_part))
 
 
@@ -91,7 +91,7 @@
 
 def polar_kernel(parts_ref, packed_ref):
     packed = jnp.sum(parts_ref[...], 0)
-    gram = unpack(packed)
+    gram = unpack(packed, jnp.float32)
     row, col, _, left = places(HALF // 2)
     diagonal = jnp.where(left, row, row + HALF // 2) == col
     trace = 2.0 * jnp.sum(jnp.where(diagonal, packed, 0.0), keepdims=True)
@@ -119,7 +119,7 @@
     first = 0
     for spot, step in enumerate(SAVES):
         for freq in range(first, first + step, 2):
-            pair = [unpack(packed_ref[freq + k]).astype(jnp.bfloat16) for k in range(2)]
+            pair = [unpack(packed_ref[freq + k], jnp.bfloat16) for k in range(2)]
             blank = jnp.zeros_like(pair[0])
             mapping = jnp.concatenate(
                 [jnp.concatenate([pair[0], blank], 1), jnp.concatenate([blank, pair[1]], 1)], 0

time: 38.2 us -> 38.2 us (level)
  no operation moved by 1% of the time
where the time goes in v6:
time: 38.2 us; the launch traced here: 38 us
  blocking collectives  28.2 us (74%)
  Pallas kernels  9.74 us (25%)
    all_to_all x1, blocking collectives, local(): parts = lax.all_to_all(packed, 'pts', 0, 0, tiled=True)  16.7 us
    all_to_all x1, blocking collectives, local(): mappings = lax.all_to_all(own, 'pts', 0, 0, tiled=True)  11.6 us
    pallas_call x1, Pallas kernels, local(): pl.pallas_call(gram_kernel, in_specs=[hbm, hbm], out_specs=[vmem, vmem],...  3.58 us
    pallas_call x1, Pallas kernels, local(): pl.pallas_call(polar_kernel, in_specs=[vmem], out_specs=vmem, out_shape=p...  3.12 us
    pallas_call x1, Pallas kernels, local(): pl.pallas_call(apply_kernel, in_specs=[vmem, vmem], out_specs=hbm, out_sh...  3.03 us

profile of v6, /device:TPU:0, one launch (start us, length us, event | category | flops | bytes accessed | tf_op | source)
XLA Modules:
  0.0 38.0 jit_solution(14637587862416310333)
XLA Ops:
  0.0 3.6 %gram.1 = (f32[16,32,128]{2,1,0:T(8,128)S(1)}, bf16[16,5,256,128]{3,2,1,0:T(8,128)(2,1)S(1)}) custom-call(bf16[16,5,256,128]{3,2,1,0:T(8,128)(2,1)} %spectra_ref.1, f32[2,128]{1,0:T(2,128)} %bitcast.1), custom_call_target="tpu_custom_call" | custom-call | tf_op jit(solution)/shard_map/gram/pallas_call | solution.py:150
  3.6 16.7 %all_to_all.10.parts_ref = f32[16,32,128]{2,1,0:T(8,128)S(1)} all-to-all(f32[16,32,128]{2,1,0:T(8,128)S(1)} %get-tuple-element.7), channel_id=1, replica_groups=mesh['pts'=16,'freq'=8] {'pts'}, dimensions={0} | all-to-all | bytes 524288 | tf_op jit(solution)/shard_map/all_to_all | solution.py:167
  20.2 3.1 %polar.1 = f32[16,32,128]{2,1,0:T(8,128)S(1)} custom-call(f32[16,32,128]{2,1,0:T(8,128)S(1)} %all_to_all.10.parts_ref), custom_call_target="tpu_custom_call" | custom-call | tf_op jit(solution)/shard_map/polar/pallas_call | solution.py:168
  23.4 11.6 %all_to_all.11.packed_ref = f32[16,32,128]{2,1,0:T(8,128)S(1)} all-to-all(f32[16,32,128]{2,1,0:T(8,128)S(1)} %polar.1), channel_id=1, replica_groups=mesh['pts'=16,'freq'=8] {'pts'}, dimensions={0} | all-to-all | bytes 524288 | tf_op jit(solution)/shard_map/all_to_all | solution.py:176
  35.0 3.0 %apply.1 = bf16[16,5,256,128]{3,2,1,0:T(8,128)(2,1)} custom-call(f32[16,32,128]{2,1,0:T(8,128)S(1)} %all_to_all.11.packed_ref, bf16[16,5,256,128]{3,2,1,0:T(8,128)(2,1)S(1)} %get-tuple-element.8.spectra_ref), custom_call_target="tpu_custom_call" | custom-call | tf_op jit(solution)/shard_map/apply/pallas_call | solution.py:177

commit v7 on v6

--- a/solution.py
+++ b/solution.py
@@ -90,7 +90,10 @@
 
 
 def polar_kernel(parts_ref, packed_ref):
-    packed = jnp.sum(parts_ref[...], 0)
+    terms = [parts_ref[spot] for spot in range(parts_ref.shape[0])]
+    while len(terms) > 1:
+        terms = [terms[spot] + terms[spot + 1] for spot in range(0, len(terms), 2)]
+    packed = terms[0]
     gram = unpack(packed, jnp.float32)
     row, col, _, left = places(HALF // 2)
     diagonal = jnp.where(left, row, row + HALF // 2) == col

time: 38.2 us -> 38.2 us (level)
  no operation moved by 1% of the time
where the time goes in v7:
time: 38.2 us; the launch traced here: 38 us
  blocking collectives  28.2 us (74%)
  Pallas kernels  9.74 us (25%)
    all_to_all x1, blocking collectives, local(): parts = lax.all_to_all(packed, 'pts', 0, 0, tiled=True)  16.7 us
    all_to_all x1, blocking collectives, local(): mappings = lax.all_to_all(own, 'pts', 0, 0, tiled=True)  11.6 us
    pallas_call x1, Pallas kernels, local(): pl.pallas_call(gram_kernel, in_specs=[hbm, hbm], out_specs=[vmem, vmem],...  3.58 us
    pallas_call x1, Pallas kernels, local(): pl.pallas_call(polar_kernel, in_specs=[vmem], out_specs=vmem, out_shape=p...  3.12 us
    pallas_call x1, Pallas kernels, local(): pl.pallas_call(apply_kernel, in_specs=[vmem, vmem], out_specs=hbm, out_sh...  3.03 us

profile of v7, /device:TPU:0, one launch (start us, length us, event | category | flops | bytes accessed | tf_op | source)
XLA Modules:
  0.0 38.0 jit_solution(9357561425263521451)
XLA Ops:
  0.0 3.6 %gram.1 = (f32[16,32,128]{2,1,0:T(8,128)S(1)}, bf16[16,5,256,128]{3,2,1,0:T(8,128)(2,1)S(1)}) custom-call(bf16[16,5,256,128]{3,2,1,0:T(8,128)(2,1)} %spectra_ref.1, f32[2,128]{1,0:T(2,128)} %bitcast.1), custom_call_target="tpu_custom_call" | custom-call | tf_op jit(solution)/shard_map/gram/pallas_call | solution.py:153
  3.6 16.7 %all_to_all.10.parts_ref = f32[16,32,128]{2,1,0:T(8,128)S(1)} all-to-all(f32[16,32,128]{2,1,0:T(8,128)S(1)} %get-tuple-element.7), channel_id=1, replica_groups=mesh['pts'=16,'freq'=8] {'pts'}, dimensions={0} | all-to-all | bytes 524288 | tf_op jit(solution)/shard_map/all_to_all | solution.py:170
  20.2 3.1 %polar.1 = f32[16,32,128]{2,1,0:T(8,128)S(1)} custom-call(f32[16,32,128]{2,1,0:T(8,128)S(1)} %all_to_all.10.parts_ref), custom_call_target="tpu_custom_call" | custom-call | tf_op jit(solution)/shard_map/polar/pallas_call | solution.py:171
  23.4 11.6 %all_to_all.11.packed_ref = f32[16,32,128]{2,1,0:T(8,128)S(1)} all-to-all(f32[16,32,128]{2,1,0:T(8,128)S(1)} %polar.1), channel_id=1, replica_groups=mesh['pts'=16,'freq'=8] {'pts'}, dimensions={0} | all-to-all | bytes 524288 | tf_op jit(solution)/shard_map/all_to_all | solution.py:179
  35.0 3.0 %apply.1 = bf16[16,5,256,128]{3,2,1,0:T(8,128)(2,1)} custom-call(f32[16,32,128]{2,1,0:T(8,128)S(1)} %all_to_all.11.packed_ref, bf16[16,5,256,128]{3,2,1,0:T(8,128)(2,1)S(1)} %get-tuple-element.8.spectra_ref), custom_call_target="tpu_custom_call" | custom-call | tf_op jit(solution)/shard_map/apply/pallas_call | solution.py:180
